TPU v7x, 32 devices: a whole 2x2x4 slice. The times are simulated.
32 devices in a mesh: interval: 4 (over y, x), slab: 8 (over z, core).
Axes of the slice: x: 2, y: 2, z: 4, core: 2. Of those that a mesh axis runs over, the one named last changes fastest.
Arguments:
- states: float32 [8, 16, 256, 512], P('interval', 'slab'), may hold values from -0.9 to 0.9
- occupations: int32 [8], P('interval'), may hold values from 1 to 64
- core_density: float32 [16, 256, 512], P('slab'), may hold values from 0.1 to 1
Outputs:
- potential: float32 [16, 256, 512], P('slab', 'interval')
All inputs are finite; a program needn't handle non-finite values.
Results may differ from a plain program's by a relative error of at most 0.00002.
Values sent between devices are 32-bit elements; how exact they have to be, the bound alone decides.
A program may use at most 64 MiB of HBM per device.

v0:
```python
import jax
import jax.numpy as jnp
from jax import lax
from jax.sharding import PartitionSpec as P

spacing = 0.25
denominator = 64.0
pbe_kappa = 0.804
pbe_mu = 0.2195149727645171
pbe_beta = 0.06672455060314922
pw_alpha = 0.0310907


def with_halo(block, sides, width):
    for axis, dim in sides:
        count = lax.axis_size(axis)
        forward = [(i, i + 1) for i in range(count - 1)]
        forward.append((count - 1, 0))
        backward = [(target, source) for source, target in forward]
        low = lax.ppermute(
            lax.slice_in_dim(block, block.shape[dim] - width, None, axis=dim), axis, forward
        )
        high = lax.ppermute(lax.slice_in_dim(block, 0, width, axis=dim), axis, backward)
        block = jnp.concatenate([low, block, high], axis=dim)
    return block


def deriv_roll(field, axis):
    near = jnp.roll(field, -1, axis) - jnp.roll(field, 1, axis)
    far = jnp.roll(field, -2, axis) - jnp.roll(field, 2, axis)
    return (8.0 * near - far) / (12.0 * spacing)


def deriv_inner(padded, axis):
    count = padded.shape[axis] - 4
    near = lax.slice_in_dim(padded, 3, 3 + count, axis=axis) - lax.slice_in_dim(
        padded, 1, 1 + count, axis=axis
    )
    far = lax.slice_in_dim(padded, 4, 4 + count, axis=axis) - lax.slice_in_dim(
        padded, 0, count, axis=axis
    )
    return (8.0 * near - far) / (12.0 * spacing)


def pbe_energy(density, grad_sq):
    pbe_gamma = (1.0 - jnp.log(2.0)) / jnp.pi**2
    k_fermi = jnp.cbrt(3.0 * jnp.pi**2 * density)
    ex_unif = -0.75 * jnp.cbrt(3.0 / jnp.pi) * jnp.cbrt(density)
    s_sq = grad_sq / (4.0 * k_fermi**2 * density**2)
    f_exch = 1.0 + pbe_kappa - pbe_kappa / (1.0 + pbe_mu * s_sq / pbe_kappa)
    radius = jnp.cbrt(3.0 / (4.0 * jnp.pi * density))
    root_r = jnp.sqrt(radius)
    lower = (
        2.0
        * pw_alpha
        * (7.5957 * root_r + 3.5876 * radius + 1.6382 * radius * root_r + 0.49294 * radius**2)
    )
    e_corr = -2.0 * pw_alpha * (1.0 + 0.2137 * radius) * jnp.log(1.0 + 1.0 / lower)
    k_screen = jnp.sqrt(4.0 * k_fermi / jnp.pi)
    t_sq = grad_sq / (4.0 * k_screen**2 * density**2)
    factor = pbe_beta / pbe_gamma / jnp.expm1(-e_corr / pbe_gamma)
    ratio_t = (1.0 + factor * t_sq) / (1.0 + factor * t_sq + factor**2 * t_sq**2)
    h_term = pbe_gamma * jnp.log(1.0 + pbe_beta / pbe_gamma * t_sq * ratio_t)
    return density * (ex_unif * f_exch + e_corr + h_term)


def local_derivs(density, grad_sq):
    return jax.grad(lambda rho, grd: jnp.sum(pbe_energy(rho, grd)), argnums=(0, 1))(
        density, grad_sq
    )


def planes_deriv(flux_z):
    padded = with_halo(flux_z, (("slab", 0),), 2)
    return deriv_inner(padded, 0)


def shards(states, occupations, core_density):
    weights = occupations.astype(jnp.float32) / denominator
    terms = weights[0] * states[0] * states[0]
    terms = terms + weights[1] * states[1] * states[1]
    share = lax.psum_scatter(terms, "interval", scatter_dimension=1, tiled=True)
    width = share.shape[1]
    start = lax.axis_index("interval") * width
    density = share + lax.dynamic_slice_in_dim(core_density, start, width, 1)
    padded = with_halo(density, (("interval", 1), ("slab", 0)), 2)
    grad_z = deriv_inner(padded[:, 2:-2], 0)
    grad_x = deriv_inner(padded[2:-2], 1)
    grad_y = deriv_roll(density, 2)
    grad_sq = grad_z * grad_z + grad_x * grad_x + grad_y * grad_y
    energy_rho, energy_grad = local_derivs(density, grad_sq)
    flux_x = with_halo(2.0 * energy_grad * grad_x, (("interval", 1),), 2)
    diverge = (
        planes_deriv(2.0 * energy_grad * grad_z)
        + deriv_inner(flux_x, 1)
        + deriv_roll(2.0 * energy_grad * grad_y, 2)
    )
    return energy_rho - diverge


def solution(mesh):
    return jax.shard_map(
        shards,
        mesh=mesh,
        in_specs=(P("interval", "slab", None, None), P("interval"), P("slab", None, None)),
        out_specs=P("slab", "interval", None),
        check_vma=False,
    )
```

profile of v0, /device:TPU:0, one launch (start us, length us, event | category | flops | bytes accessed | tf_op | source)
XLA Modules:
  0.0 81.9 jit_solution(12330501609096962924)
XLA Ops:
  6.5 0.7 convert_multiply_fusion
  7.2 0.6 fusion.54
  7.8 4.0 %fusion = f32[2,256,512]{2,1,0:T(8,128)} fusion(f32[2,2,256,512]{3,2,1,0:T(8,128)} %param.3, f32[]{:T(128)} %bitcast.2, f32[]{:T(128)} %bitcast), kind=kLoop, calls=%fused_computation.2 | loop fusion | flops 1310720 | bytes 3145736 | tf_op jit(solution)/shard_map/add | solution.py:81
  11.7 30.8 %reduce-scatter.2.cloned.1.call-done = f32[2,64,512]{2,1,0:T(8,128)} async-done(((f32[2,256,512]{2,1,0:T(8,128)}), f32[2,64,512]{2,1,0:T(8,128)}) %reduce-scatter.2.cloned.1.call-update) | async-done | bytes 262160 | tf_op jit(solution)/shard_map/reduce_scatter | solution.py:82
  42.6 1.1 %dynamic-slice_add_fusion = f32[2,64,512]{2,1,0:T(8,128)S(1)} fusion(f32[2,64,512]{2,1,0:T(8,128)} %reduce-scatter.2.cloned.1.call-done, f32[2,256,512]{2,1,0:T(8,128)} %param.5, s32[]{:T(128)S(6)} %select_n.3), kind=kLoop, calls=%fused_computation.84 | loop fusion | flops 65536 | bytes 786436 | tf_op jit(solution)/shard_map/add | solution.py:85
  43.7 0.1 fusion.49
  43.8 1.5 %collective-permute-start = (f32[2,2,512]{2,1,0:T(2,128)S(1)}, f32[2,2,512]{2,1,0:T(2,128)S(1)}, u32[]{:S(2)}, u32[]{:S(2)}) collective-permute-start(f32[2,2,512]{2,1,0:T(2,128)S(1)} %get-tuple-element.30), channel_id=1, source_target_pairs={{0,8},{8,16},{16,24},{24,0},{1,9},{9,17},{17,25},{25,1},{2,10},{10... | collective-permute-start | bytes 24584 | tf_op jit(solution)/shard_map/ppermute | solution.py:20
  45.3 1.5 %collective-permute-start.1 = (f32[2,2,512]{2,1,0:T(2,128)S(1)}, f32[2,2,512]{2,1,0:T(2,128)S(1)}, u32[]{:S(2)}, u32[]{:S(2)}) collective-permute-start(f32[2,2,512]{2,1,0:T(2,128)S(1)} %get-tuple-element.31), channel_id=1, source_target_pairs={{8,0},{16,8},{24,16},{0,24},{9,1},{17,9},{25,17},{1,25},{10,2},{18... | collective-permute-start | bytes 24584 | tf_op jit(solution)/shard_map/ppermute | solution.py:23
  46.8 0.1 fusion.50
  46.9 1.5 %collective-permute-done = f32[2,2,512]{2,1,0:T(2,128)S(1)} collective-permute-done((f32[2,2,512]{2,1,0:T(2,128)S(1)}, f32[2,2,512]{2,1,0:T(2,128)S(1)}, u32[]{:S(2)}, u32[]{:S(2)}) %collective-permute-start) | collective-permute-done | bytes 8224 | tf_op jit(solution)/shard_map/ppermute | solution.py:20
  48.4 0.6 collective-permute-done.1
  49.1 3.5 %collective-permute-start.2 = (f32[2,68,512]{2,1,0:T(8,128)S(1)}, f32[2,68,512]{2,1,0:T(8,128)S(1)}, u32[]{:S(2)}, u32[]{:S(2)}) collective-permute-start(f32[2,68,512]{2,1,0:T(8,128)S(1)} %pad_maximum_fusion), channel_id=1, source_target_pairs={{1,0},{2,1},{3,2},{4,3},{5,4},{6,5},{7,6},{0,7},{9,8},{10,9},{11,1... | collective-permute-start | bytes 835592 | tf_op jit(solution)/shard_map/ppermute | solution.py:23
  52.6 0.1 fusion.52
  52.7 0.1 fusion.51
  52.8 5.5 %collective-permute-done.3 = f32[2,68,512]{2,1,0:T(8,128)S(1)} collective-permute-done((f32[2,68,512]{2,1,0:T(8,128)S(1)}, f32[2,68,512]{2,1,0:T(8,128)S(1)}, u32[]{:S(2)}, u32[]{:S(2)}) %collective-permute-start.3) | collective-permute-done | bytes 278560 | tf_op jit(solution)/shard_map/ppermute | solution.py:20
  58.3 2.0 %fusion.39 = (f32[2,64,512]{2,1,0:T(8,128)S(1)}, f32[2,64,512]{2,1,0:T(8,128)S(1)}, f32[2,64,512]{2,1,0:T(8,128)S(1)}, f32[2,64,512]{2,1,0:T(8,128)S(1)}, f32[2,64,512]{2,1,0:T(8,128)S(1)}) fusion(f32[2,64,512]{2,1,0:T(8,128)S(1)} %dynamic-slice_add_fusion, f32[2,68,512]{2,1,0:T(8,128)S(1)} %collective-permute-done.3, ...), kind=kLoop, calls=%fused_computation.89 | loop fusion | flops 7274496 | bytes 4014080 | tf_op jit(solution)/shard_map/mul | solution.py:96
  60.4 1.7 %collective-permute-start.5 = (f32[2,64,512]{2,1,0:T(8,128)S(1)}, f32[2,64,512]{2,1,0:T(8,128)S(1)}, u32[]{:S(2)}, u32[]{:S(2)}) collective-permute-start(f32[2,64,512]{2,1,0:T(8,128)S(1)} %get-tuple-element.18), channel_id=1, source_target_pairs={{0,1},{1,2},{2,3},{3,4},{4,5},{5,6},{6,7},{7,0},{8,9},{9,10},{10,1... | collective-permute-start | bytes 786440 | tf_op jit(solution)/shard_map/ppermute | solution.py:20
  62.1 1.9 %collective-permute-start.4 = (f32[2,64,512]{2,1,0:T(8,128)S(1)}, f32[2,64,512]{2,1,0:T(8,128)S(1)}, u32[]{:S(2)}, u32[]{:S(2)}) collective-permute-start(f32[2,64,512]{2,1,0:T(8,128)S(1)} %get-tuple-element.18), channel_id=1, source_target_pairs={{1,0},{2,1},{3,2},{4,3},{5,4},{6,5},{7,6},{0,7},{9,8},{10,9},{11,1... | collective-permute-start | bytes 786440 | tf_op jit(solution)/shard_map/ppermute | solution.py:23
  64.1 0.1 fusion.46
  64.2 0.1 fusion.44
  64.4 2.4 %collective-permute-start.6 = (f32[2,2,512]{2,1,0:T(2,128)S(1)}, f32[2,2,512]{2,1,0:T(2,128)S(1)}, u32[]{:S(2)}, u32[]{:S(2)}) collective-permute-start(f32[2,2,512]{2,1,0:T(2,128)S(1)} %get-tuple-element.20), channel_id=1, source_target_pairs={{8,0},{16,8},{24,16},{0,24},{9,1},{17,9},{25,17},{1,25},{10,2},{18... | collective-permute-start | bytes 24584 | tf_op jit(solution)/shard_map/ppermute | solution.py:23
  66.9 1.5 %collective-permute-done.6 = f32[2,2,512]{2,1,0:T(2,128)S(1)} collective-permute-done((f32[2,2,512]{2,1,0:T(2,128)S(1)}, f32[2,2,512]{2,1,0:T(2,128)S(1)}, u32[]{:S(2)}, u32[]{:S(2)}) %collective-permute-start.6) | collective-permute-done | bytes 8224 | tf_op jit(solution)/shard_map/ppermute | solution.py:23
  68.4 2.9 %collective-permute-done.7 = f32[2,2,512]{2,1,0:T(2,128)S(1)} collective-permute-done((f32[2,2,512]{2,1,0:T(2,128)S(1)}, f32[2,2,512]{2,1,0:T(2,128)S(1)}, u32[]{:S(2)}, u32[]{:S(2)}) %collective-permute-start.7) | collective-permute-done | bytes 8224 | tf_op jit(solution)/shard_map/ppermute | solution.py:20
  71.4 3.7 %fusion.8 = f32[2,64,512]{2,1,0:T(8,128)} fusion(f32[2,2,512]{2,1,0:T(2,128)S(1)} %collective-permute-done.7, f32[2,64,512]{2,1,0:T(8,128)S(1)} %get-tuple-element.19, f32[2,2,512]{2,1,0:T(2,128)S(1)} %collective-permute-done.6, f32[2,64,512]{2,1,0:T(8,128)S(1)} %get-tuple-element.18, f32[2,64,512]{2,1,0:T(8,128)S(1)} %collective-permute-done.5, ...), kind=kLoop, calls=%fused_computation.19 | loop fusion | flops 13107200 | bytes 3424256 | tf_op jit(solution)/shard_map/sub | solution.py:98
  (13 shorter events, 0.4 us)
Async XLA Ops:
  6.5 36.0 %reduce-scatter.2.cloned.1.call-start = ((), (), s32[]{:S(2)}) async-start(), calls=%async_computation.1 | async-start | bytes 1310720 | tf_op jit(solution)/shard_map/reduce_scatter | solution.py:82
  43.8 4.6 %collective-permute-start = (f32[2,2,512]{2,1,0:T(2,128)S(1)}, f32[2,2,512]{2,1,0:T(2,128)S(1)}, u32[]{:S(2)}, u32[]{:S(2)}) collective-permute-start(f32[2,2,512]{2,1,0:T(2,128)S(1)} %get-tuple-element.30), channel_id=1, source_target_pairs={{0,8},{8,16},{16,24},{24,0},{1,9},{9,17},{17,25},{25,1},{2,10},{10... | collective-permute-start | bytes 24584 | tf_op jit(solution)/shard_map/ppermute | solution.py:20
  45.3 3.7 %collective-permute-start.1 = (f32[2,2,512]{2,1,0:T(2,128)S(1)}, f32[2,2,512]{2,1,0:T(2,128)S(1)}, u32[]{:S(2)}, u32[]{:S(2)}) collective-permute-start(f32[2,2,512]{2,1,0:T(2,128)S(1)} %get-tuple-element.31), channel_id=1, source_target_pairs={{8,0},{16,8},{24,16},{0,24},{9,1},{17,9},{25,17},{1,25},{10,2},{18... | collective-permute-start | bytes 24584 | tf_op jit(solution)/shard_map/ppermute | solution.py:23
  49.0 9.3 %collective-permute-start.3 = (f32[2,68,512]{2,1,0:T(8,128)S(1)}, f32[2,68,512]{2,1,0:T(8,128)S(1)}, u32[]{:S(2)}, u32[]{:S(2)}) collective-permute-start(f32[2,68,512]{2,1,0:T(8,128)S(1)} %pad_maximum_fusion), channel_id=1, source_target_pairs={{0,1},{1,2},{2,3},{3,4},{4,5},{5,6},{6,7},{7,0},{8,9},{9,10},{10,1... | collective-permute-start | bytes 835592 | tf_op jit(solution)/shard_map/ppermute | solution.py:20
  49.1 9.3 %collective-permute-start.2 = (f32[2,68,512]{2,1,0:T(8,128)S(1)}, f32[2,68,512]{2,1,0:T(8,128)S(1)}, u32[]{:S(2)}, u32[]{:S(2)}) collective-permute-start(f32[2,68,512]{2,1,0:T(8,128)S(1)} %pad_maximum_fusion), channel_id=1, source_target_pairs={{1,0},{2,1},{3,2},{4,3},{5,4},{6,5},{7,6},{0,7},{9,8},{10,9},{11,1... | collective-permute-start | bytes 835592 | tf_op jit(solution)/shard_map/ppermute | solution.py:23
  60.4 11.0 %collective-permute-start.5 = (f32[2,64,512]{2,1,0:T(8,128)S(1)}, f32[2,64,512]{2,1,0:T(8,128)S(1)}, u32[]{:S(2)}, u32[]{:S(2)}) collective-permute-start(f32[2,64,512]{2,1,0:T(8,128)S(1)} %get-tuple-element.18), channel_id=1, source_target_pairs={{0,1},{1,2},{2,3},{3,4},{4,5},{5,6},{6,7},{7,0},{8,9},{9,10},{10,1... | collective-permute-start | bytes 786440 | tf_op jit(solution)/shard_map/ppermute | solution.py:20
  62.1 9.3 %collective-permute-start.4 = (f32[2,64,512]{2,1,0:T(8,128)S(1)}, f32[2,64,512]{2,1,0:T(8,128)S(1)}, u32[]{:S(2)}, u32[]{:S(2)}) collective-permute-start(f32[2,64,512]{2,1,0:T(8,128)S(1)} %get-tuple-element.18), channel_id=1, source_target_pairs={{1,0},{2,1},{3,2},{4,3},{5,4},{6,5},{7,6},{0,7},{9,8},{10,9},{11,1... | collective-permute-start | bytes 786440 | tf_op jit(solution)/shard_map/ppermute | solution.py:23
  64.4 4.1 %collective-permute-start.6 = (f32[2,2,512]{2,1,0:T(2,128)S(1)}, f32[2,2,512]{2,1,0:T(2,128)S(1)}, u32[]{:S(2)}, u32[]{:S(2)}) collective-permute-start(f32[2,2,512]{2,1,0:T(2,128)S(1)} %get-tuple-element.20), channel_id=1, source_target_pairs={{8,0},{16,8},{24,16},{0,24},{9,1},{17,9},{25,17},{1,25},{10,2},{18... | collective-permute-start | bytes 24584 | tf_op jit(solution)/shard_map/ppermute | solution.py:23
  66.8 4.5 %collective-permute-start.7 = (f32[2,2,512]{2,1,0:T(2,128)S(1)}, f32[2,2,512]{2,1,0:T(2,128)S(1)}, u32[]{:S(2)}, u32[]{:S(2)}) collective-permute-start(f32[2,2,512]{2,1,0:T(2,128)S(1)} %get-tuple-element.21), channel_id=1, source_target_pairs={{0,8},{8,16},{16,24},{24,0},{1,9},{9,17},{17,25},{25,1},{2,10},{10... | collective-permute-start | bytes 24584 | tf_op jit(solution)/shard_map/ppermute | solution.py:20
Sparse Core Ops, SparseCore 0:
  11.9 30.6 reduce-scatter.1
where the time goes:
time: 82.1 us; the launch traced here: 81.9 us
  waiting for transfers between devices  42.9 us (52%)
  between operations  13.5 us (16%)
  starting transfers between devices  12.6 us (15%)
  other arithmetic  11.5 us (14%)
  local copies, waits for them, and re-layouts  1.43 us (2%)
    reduce_scatter x1, waiting for transfers between devices, shards(): share = lax.psum_scatter(terms, 'interval', scatter_dimension=1, tiled=True)  30.8 us
    ppermute x4, waiting for transfers between devices, with_halo(): lax.ppermute(lax.slice_in_dim(block, block.shape[dim] - width, None, axis...  9.99 us
    ppermute x4, starting transfers between devices, with_halo(): lax.ppermute(lax.slice_in_dim(block, 0, width, axis=dim), axis, backward)  9.35 us
    add x1, other arithmetic, shards(): terms = terms + weights[1] * states[1] * states[1]  3.97 us
    sub x1, other arithmetic, shards(): return energy_rho - diverge  3.7 us
    ppermute x4, starting transfers between devices, with_halo(): lax.ppermute(lax.slice_in_dim(block, block.shape[dim] - width, None, axis...  3.3 us
    ppermute x4, waiting for transfers between devices, with_halo(): lax.ppermute(lax.slice_in_dim(block, 0, width, axis=dim), axis, backward)  2.04 us
    mul x1, other arithmetic, shards(): 2.0 * energy_grad * grad_y  2 us
  transfers between devices with their start and end apart: 9, of which 6 were waited for; matrix products, arithmetic and copies ran while one was open for 1% of the time, Pallas kernels for 0%

commit v1 on v0

v1 whole, which is shorter than its diff:
```python
import functools
import math

import jax
import jax.numpy as jnp
from jax import lax
from jax.experimental import pallas as pl
from jax.experimental.pallas import tpu as pltpu
from jax.sharding import PartitionSpec as P

spacing = 0.25
denominator = 64.0
pbe_kappa = 0.804
pbe_mu = 0.2195149727645171
pbe_beta = 0.06672455060314922
pw_alpha = 0.0310907
pbe_gamma = (1.0 - math.log(2.0)) / math.pi**2
MESH = pl.DeviceIdType.MESH
edge = 8


def five_point(low2, low1, high1, high2):
    return (8.0 * (high1 - low1) - (high2 - low2)) * (1.0 / (12.0 * spacing))


def deriv_y(field):
    axis = field.ndim - 1
    count = field.shape[axis]
    return five_point(
        pltpu.roll(field, 2, axis),
        pltpu.roll(field, 1, axis),
        pltpu.roll(field, count - 1, axis),
        pltpu.roll(field, count - 2, axis),
    )


def deriv_x(tall):
    return five_point(
        tall[:, edge - 2 : -edge - 2],
        tall[:, edge - 1 : -edge - 1],
        tall[:, edge + 1 : 1 - edge],
        tall[:, edge + 2 : 2 - edge],
    )


def deriv_z(tall):
    count = tall.shape[0] - 4
    return five_point(
        tall[:count], tall[1 : count + 1], tall[3 : count + 3], tall[4 : count + 4]
    )


def pbe_derivs(n, g):
    k_one = (3.0 * math.pi**2) ** (1.0 / 3.0)
    ex_one = -0.75 * (3.0 / math.pi) ** (1.0 / 3.0)
    r_one = (3.0 / (4.0 * math.pi)) ** (1.0 / 3.0)
    s_one = 1.0 / (4.0 * k_one**2)
    t_one = math.pi / (16.0 * k_one)
    ratio = pbe_beta / pbe_gamma
    inv_six = jnp.exp(jnp.log(n) * (-1.0 / 6.0))
    inv = inv_six * inv_six
    inv2 = inv * inv
    inv4 = inv2 * inv2
    cube = n * inv2
    s_sq = (s_one * g) * (inv4 * inv4)
    u_inv = 1.0 / (1.0 + (pbe_mu / pbe_kappa) * s_sq)
    f_exch = (1.0 + pbe_kappa) - pbe_kappa * u_inv
    f_slope = pbe_mu * u_inv * u_inv
    ex_rho = (ex_one * cube) * ((4.0 / 3.0) * f_exch - (8.0 / 3.0) * f_slope * s_sq)

    radius = r_one * inv
    root = math.sqrt(r_one) * inv_six
    two_a = 2.0 * pw_alpha
    lower = (two_a * root) * (
        7.5957 + root * (3.5876 + root * (1.6382 + root * 0.49294))
    )
    slope = (two_a * root) * (
        0.5 * 7.5957 + root * (3.5876 + root * (1.5 * 1.6382 + root * (2.0 * 0.49294)))
    )
    pair_inv = 1.0 / (lower * (lower + 1.0))
    log_term = jnp.log(1.0 + (lower + 1.0) * pair_inv)
    front = two_a + (two_a * 0.2137) * radius
    e_corr = -front * log_term
    n_ec = (1.0 / 3.0) * ((two_a * 0.2137) * radius * log_term - front * slope * pair_inv)

    grown = jnp.exp(e_corr * (-1.0 / pbe_gamma))
    factor = ratio / (grown - 1.0)
    t_sq = (t_one * g) * (inv4 * inv2 * inv)
    y = factor * t_sq
    lift = 1.0 + y
    den = lift + y * y
    add = (ratio * t_sq) * lift
    full = den + add
    inv_full = 1.0 / (den * full)
    h_term = pbe_gamma * jnp.log(1.0 + add * (full * inv_full))
    h_t = (pbe_beta * inv_full) * (1.0 + 2.0 * y)
    h_ec = -(y * y) * (y * (2.0 + y)) * inv_full * grown
    e_rho = ex_rho + e_corr + h_term + n_ec + h_ec * n_ec - (7.0 / 3.0) * (t_sq * h_t)
    e_grad = inv4 * (t_one * h_t + (ex_one * s_one) * f_slope)
    return e_rho, e_grad


def kernel(
    peers, slabs, rows,
    states, occ, core, out,
    stage, core_v, snd, rcv, dens, fz, fx,
    in_sem, core_sem, rs_send, rs_recv, z_send, z_recv, x_send, x_recv,
):
    nst, nz, wide = stage.shape[1], stage.shape[2], stage.shape[3]
    chunks = wide // rows
    me = lax.axis_index("interval")
    sl = lax.axis_index("slab")
    z_low = lax.rem(sl + slabs - 1, slabs)
    z_high = lax.rem(sl + 1, slabs)
    x_low = lax.rem(me + peers - 1, peers)
    x_high = lax.rem(me + 1, peers)
    order = [0] + ([chunks - 1] if chunks > 1 else []) + list(range(1, chunks - 1))

    def pull(k, c):
        start = pl.multiple_of(lax.rem(me + k, peers) * wide + c * rows, 8)
        return pltpu.make_async_copy(
            states.at[:, :, pl.ds(start, rows), :],
            stage.at[k, :, :, pl.ds(c * rows, rows), :],
            in_sem.at[k, c],
        )

    for c in order:
        for k in [*range(1, peers), 0]:
            pull(k, c).start()
    core_copy = pltpu.make_async_copy(
        core.at[:, pl.ds(pl.multiple_of(me * wide, 8), wide), :], core_v, core_sem
    )
    core_copy.start()

    barrier = pltpu.get_barrier_semaphore()
    for k in range(1, peers):
        pl.semaphore_signal(
            barrier, inc=1, device_id=(lax.rem(me + k, peers), sl), device_id_type=MESH
        )
    for z in (z_low, z_high):
        pl.semaphore_signal(barrier, inc=1, device_id=(me, z), device_id_type=MESH)

    weights = [occ[s].astype(jnp.float32) * (1.0 / denominator) for s in range(nst)]

    def term(k, at):
        total = None
        for s in range(nst):
            value = stage[k, s, :, pl.ds(at, edge), :]
            part = (weights[s] * value) * value
            total = part if total is None else total + part
        return total

    def tiles(c, body):
        def step(t, _):
            body(pl.multiple_of(c * rows + t * edge, edge))
            return 0

        lax.fori_loop(0, rows // edge, step, 0)

    def share(k, c):
        span = pl.ds(c * rows, rows)
        return pltpu.make_async_remote_copy(
            src_ref=snd.at[k - 1, :, span, :],
            dst_ref=rcv.at[k - 1, :, span, :],
            send_sem=rs_send.at[k - 1, c],
            recv_sem=rs_recv.at[k - 1, c],
            device_id=(lax.rem(me + k, peers), sl),
            device_id_type=MESH,
        )

    def planes(field, way, c):
        ref = (dens, fz)[field]
        pad = (edge, 0)[field]
        span = pl.ds(pad + c * rows, rows)
        source, target = ((2, nz + 2), (nz, 0))[way]
        return pltpu.make_async_remote_copy(
            src_ref=ref.at[pl.ds(source, 2), span, :],
            dst_ref=ref.at[pl.ds(target, 2), span, :],
            send_sem=z_send.at[field, way, c],
            recv_sem=z_recv.at[field, way, c],
            device_id=(me, (z_low, z_high)[way]),
            device_id_type=MESH,
        )

    def sides(field, way):
        ref = (dens.at[pl.ds(2, nz)], fx)[field]
        source, target = ((edge, edge + wide), (wide, 0))[way]
        return pltpu.make_async_remote_copy(
            src_ref=ref.at[:, pl.ds(source, edge), :],
            dst_ref=ref.at[:, pl.ds(target, edge), :],
            send_sem=x_send.at[field, way],
            recv_sem=x_recv.at[field, way],
            device_id=((x_low, x_high)[way], sl),
            device_id_type=MESH,
        )

    started = []

    def start(copy):
        copy.start()
        started.append(copy)

    first = True
    for c in order:
        for k in range(1, peers):
            pull(k, c).wait()

            def fill(at, k=k):
                snd[k - 1, :, pl.ds(at, edge), :] = term(k, at)

            tiles(c, fill)
            if first:
                pl.semaphore_wait(barrier, peers + 1)
                first = False
            start(share(k, c))
    core_copy.wait()

    def gather(c):
        pull(0, c).wait()
        for k in range(1, peers):
            share(k, c).wait_recv()

        def add(at):
            total = term(0, at)
            for k in range(1, peers):
                total = total + rcv[k - 1, :, pl.ds(at, edge), :]
            dens[2 : nz + 2, pl.ds(at + edge, edge), :] = (
                total + core_v[:, pl.ds(at, edge), :]
            )

        tiles(c, add)
        if c == 0:
            start(sides(0, 0))
        if c == chunks - 1:
            start(sides(0, 1))
        for way in (0, 1):
            start(planes(0, way, c))

    def energy(c):
        for way in (0, 1):
            planes(0, way, c).wait_recv()
        if c == chunks - 1:
            sides(0, 0).wait_recv()
        if c == 0:
            sides(0, 1).wait_recv()

        def work(at):
            inner = pl.ds(at + edge, edge)
            n = dens[2 : nz + 2, inner, :]
            grad_z = deriv_z(dens[:, inner, :])
            grad_x = deriv_x(dens[2 : nz + 2, pl.ds(at, 3 * edge), :])
            grad_y = deriv_y(n)
            g = grad_z * grad_z + grad_x * grad_x + grad_y * grad_y
            e_rho, e_grad = pbe_derivs(n, g)
            twice = 2.0 * e_grad
            fz[2 : nz + 2, pl.ds(at, edge), :] = twice * grad_z
            fx[:, inner, :] = twice * grad_x
            out[:, pl.ds(at, edge), :] = e_rho - deriv_y(twice * grad_y)

        tiles(c, work)
        if c == 0:
            start(sides(1, 0))
        if c == chunks - 1:
            start(sides(1, 1))
        for way in (0, 1):
            start(planes(1, way, c))

    def diverge(c):
        for way in (0, 1):
            planes(1, way, c).wait_recv()
        if c == chunks - 1:
            sides(1, 0).wait_recv()
        if c == 0:
            sides(1, 1).wait_recv()

        def work(at):
            span = pl.ds(at, edge)
            out[:, span, :] = out[:, span, :] - (
                deriv_z(fz[:, span, :]) + deriv_x(fx[:, pl.ds(at, 3 * edge), :])
            )

        tiles(c, work)

    gathered, done = set(), set()
    for c in order:
        gather(c)
        gathered.add(c)
        for d in order:
            near = {e for e in (d - 1, d, d + 1) if 0 <= e < chunks}
            ends = d not in (0, chunks - 1) or {0, chunks - 1} <= gathered
            if d not in done and near <= gathered and ends and len(gathered) > 2:
                energy(d)
                done.add(d)
                break
    for d in order:
        if d not in done:
            energy(d)
    for d in order:
        diverge(d)
    for copy in started:
        copy.wait_send()


def shards(peers, slabs, states, occupations, core_density):
    nst, nz, full, deep = states.shape
    wide = full // peers
    rows = 16 if wide % 16 == 0 else 8
    chunks = wide // rows
    f32 = jnp.float32
    dma = pltpu.SemaphoreType.DMA
    return pl.pallas_call(
        functools.partial(kernel, peers, slabs, rows),
        out_shape=jax.ShapeDtypeStruct((nz, wide, deep), f32),
        in_specs=[
            pl.BlockSpec(memory_space=pl.ANY),
            pl.BlockSpec(memory_space=pltpu.SMEM),
            pl.BlockSpec(memory_space=pl.ANY),
        ],
        out_specs=pl.BlockSpec(memory_space=pltpu.VMEM),
        scratch_shapes=[
            pltpu.VMEM((peers, nst, nz, wide, deep), f32),
            pltpu.VMEM((nz, wide, deep), f32),
            pltpu.VMEM((peers - 1, nz, wide, deep), f32),
            pltpu.VMEM((peers - 1, nz, wide, deep), f32),
            pltpu.VMEM((nz + 4, wide + 2 * edge, deep), f32),
            pltpu.VMEM((nz + 4, wide, deep), f32),
            pltpu.VMEM((nz, wide + 2 * edge, deep), f32),
            dma((peers, chunks)),
            dma,
            dma((peers - 1, chunks)),
            dma((peers - 1, chunks)),
            dma((2, 2, chunks)),
            dma((2, 2, chunks)),
            dma((2, 2)),
            dma((2, 2)),
        ],
        compiler_params=pltpu.CompilerParams(
            collective_id=0, has_side_effects=True, vmem_limit_bytes=48 * 1024 * 1024
        ),
    )(states, occupations, core_density)


def solution(mesh):
    return jax.shard_map(
        functools.partial(shards, mesh.shape["interval"], mesh.shape["slab"]),
        mesh=mesh,
        in_specs=(P("interval", "slab", None, None), P("interval"), P("slab", None, None)),
        out_specs=P("slab", "interval", None),
        check_vma=False,
    )
```

time: 82.1 us -> 35.6 us (0.43)
  waiting for transfers between devices: 42.9 us -> 0 us
  Pallas kernels: 0 us -> 31.2 us
  between operations: 13.5 us -> 0.01 us
  starting transfers between devices: 12.6 us -> 0 us
  other arithmetic: 11.5 us -> 0 us
  local copies, waits for them, and re-layouts: 1.43 us -> 4.17 us
    pallas_call x0 -> x1, Pallas kernels: none -> 31.2 us  [shards(): pl.pallas_call(functools.partial(kernel, peers, slabs, rows), out_shape=j...]
    reduce_scatter x1 -> x0, waiting for transfers between devices: 30.8 us -> none  [shards(): share = lax.psum_scatter(terms, 'interval', scatter_dimension=1, tiled=True)]
    ppermute x8 -> x0, starting transfers between devices: 12.6 us -> none  [the longest x4 9.35 us: with_halo(): lax.ppermute(lax.slice_in_dim(block, 0, width, axis=dim), axis, backward)]
    ppermute x8 -> x0, waiting for transfers between devices: 12 us -> none  [the longest x4 9.99 us: with_halo(): lax.ppermute(lax.slice_in_dim(block, block.shape[dim] - width, None, axis...]
    add x2 -> x0, other arithmetic: 5.03 us -> none  [the longest x1 3.97 us: shards(): terms = terms + weights[1] * states[1] * states[1]]
    unnamed x0 -> x7, local copies, waits for them, and re-layouts: none -> 4.17 us
    sub x1 -> x0, other arithmetic: 3.7 us -> none  [shards(): return energy_rho - diverge]
    mul x2 -> x0, other arithmetic: 2.06 us -> none  [the longest x1 2 us: shards(): 2.0 * energy_grad * grad_y]
  transfers between devices with their start and end apart: 9 -> 0, of which waited for: 6 -> 0; matrix products, arithmetic and copies ran while one was open for 1% -> 0% of each run, Pallas kernels for 0% -> 0%
where the time goes in v1:
time: 35.6 us; the launch traced here: 35.4 us
  Pallas kernels  31.2 us (88%)
  local copies, waits for them, and re-layouts  4.17 us (12%)
    pallas_call x1, Pallas kernels, shards(): pl.pallas_call(functools.partial(kernel, peers, slabs, rows), out_shape=j...  31.2 us
    unnamed x7, local copies, waits for them, and re-layouts  4.17 us

profile of v1, /device:TPU:0, one launch (start us, length us, event | category | flops | bytes accessed | tf_op | source)
XLA Modules:
  0.0 35.4 jit_solution(14431460574155338098)
XLA Ops:
  0.0 0.0 copy-start
  0.0 1.6 %copy-done = f32[2,2,256,512]{3,2,1,0:T(8,128)S(1)} copy-done((f32[2,2,256,512]{3,2,1,0:T(8,128)S(1)}, f32[2,2,256,512]{3,2,1,0:T(8,128)}, u32[]{:S(2)}) %copy-start) | copy-done | bytes 2097176
  1.6 0.0 copy-start.1
  1.6 1.2 %copy-done.1 = f32[2,256,512]{2,1,0:T(8,128)S(1)} copy-done((f32[2,256,512]{2,1,0:T(8,128)S(1)}, f32[2,256,512]{2,1,0:T(8,128)}, u32[]{:S(2)}) %copy-start.1) | copy-done | bytes 1048600
  2.8 0.0 copy-start.2
  2.8 0.7 %copy-done.2 = s32[2]{0:T(128)S(1)} copy-done((s32[2]{0:T(128)S(1)}, s32[2]{0:T(128)}, u32[]{:S(2)}) %copy-start.2) | copy-done | bytes 32
  3.5 31.2 %shard_map.37 = f32[2,64,512]{2,1,0:T(8,128)S(1)} custom-call(f32[2,2,256,512]{3,2,1,0:T(8,128)S(1)} %copy-done, s32[2]{0:T(128)S(1)} %copy-done.2, f32[2,256,512]{2,1,0:T(8,128)S(1)} %copy-done.1), custom_call_target="tpu_custom_call" | custom-call | tf_op jit(solution)/shard_map/pallas_call | solution.py:311
  34.7 0.7 %copy.5 = f32[2,64,512]{2,1,0:T(8,128)} copy(f32[2,64,512]{2,1,0:T(8,128)S(1)} %shard_map.37) | data formatting | bytes 524288
Async XLA Ops:
  0.0 1.6 %copy-start = (f32[2,2,256,512]{3,2,1,0:T(8,128)S(1)}, f32[2,2,256,512]{3,2,1,0:T(8,128)}, u32[]{:S(2)}) copy-start(f32[2,2,256,512]{3,2,1,0:T(8,128)} %states.1) | copy-start | bytes 6291460
  1.6 1.2 %copy-start.1 = (f32[2,256,512]{2,1,0:T(8,128)S(1)}, f32[2,256,512]{2,1,0:T(8,128)}, u32[]{:S(2)}) copy-start(f32[2,256,512]{2,1,0:T(8,128)} %core.1) | copy-start | bytes 3145732
  2.8 0.7 %copy-start.2 = (s32[2]{0:T(128)S(1)}, s32[2]{0:T(128)}, u32[]{:S(2)}) copy-start(s32[2]{0:T(128)} %occ.1) | copy-start | bytes 28

commit v2 on v1

--- a/solution.py
+++ b/solution.py
@@ -304,7 +304,7 @@
 def shards(peers, slabs, states, occupations, core_density):
     nst, nz, full, deep = states.shape
     wide = full // peers
-    rows = 16 if wide % 16 == 0 else 8
+    rows = edge
     chunks = wide // rows
     f32 = jnp.float32
     dma = pltpu.SemaphoreType.DMA
@@ -335,7 +335,7 @@
             dma((2, 2)),
         ],
         compiler_params=pltpu.CompilerParams(
-            collective_id=0, has_side_effects=True, vmem_limit_bytes=48 * 1024 * 1024
+            collective_id=0, has_side_effects=True, vmem_limit_bytes=67043328
         ),
     )(states, occupations, core_density)
 

time: 35.6 us -> 40.4 us (1.13)
  Pallas kernels: 31.2 us -> 38.6 us
  local copies, waits for them, and re-layouts: 4.17 us -> 1.67 us
    pallas_call x1, Pallas kernels: 31.2 us -> 38.6 us  [shards(): pl.pallas_call(functools.partial(kernel, peers, slabs, rows), out_shape=j...]
    unnamed x7 -> x1, local copies, waits for them, and re-layouts: 4.17 us -> 1.67 us
where the time goes in v2:
time: 40.4 us; the launch traced here: 40.2 us
  Pallas kernels  38.6 us (96%)
  local copies, waits for them, and re-layouts  1.67 us (4%)
    pallas_call x1, Pallas kernels, shards(): pl.pallas_call(functools.partial(kernel, peers, slabs, rows), out_shape=j...  38.6 us
    unnamed x1, local copies, waits for them, and re-layouts  1.67 us

profile of v2, /device:TPU:0, one launch (start us, length us, event | category | flops | bytes accessed | tf_op | source)
XLA Modules:
  0.0 40.2 jit_solution(16787837910171075128)
XLA Ops:
  0.0 38.6 %shard_map.37 = f32[2,64,512]{2,1,0:T(8,128)} custom-call(f32[2,2,256,512]{3,2,1,0:T(8,128)} %states.1, s32[2]{0:T(128)} %occ.1, f32[2,256,512]{2,1,0:T(8,128)} %core.1), custom_call_target="tpu_custom_call" | custom-call | tf_op jit(solution)/shard_map/pallas_call | solution.py:311
  38.6 1.7 %copy.5 = f32[2,64,512]{2,1,0:T(8,128)} copy(f32[2,64,512]{2,1,0:T(8,128)} %shard_map.37) | data formatting | bytes 524288

commit v3 on v1

--- a/solution.py
+++ b/solution.py
@@ -116,17 +116,14 @@
     x_high = lax.rem(me + 1, peers)
     order = [0] + ([chunks - 1] if chunks > 1 else []) + list(range(1, chunks - 1))
 
-    def pull(k, c):
-        start = pl.multiple_of(lax.rem(me + k, peers) * wide + c * rows, 8)
+    def pull(k):
+        start = pl.multiple_of(lax.rem(me + k, peers) * wide, 8)
         return pltpu.make_async_copy(
-            states.at[:, :, pl.ds(start, rows), :],
-            stage.at[k, :, :, pl.ds(c * rows, rows), :],
-            in_sem.at[k, c],
-        )
-
-    for c in order:
-        for k in [*range(1, peers), 0]:
-            pull(k, c).start()
+            states.at[:, :, pl.ds(start, wide), :], stage.at[k], in_sem.at[k]
+        )
+
+    for k in [*range(1, peers), 0]:
+        pull(k).start()
     core_copy = pltpu.make_async_copy(
         core.at[:, pl.ds(pl.multiple_of(me * wide, 8), wide), :], core_v, core_sem
     )
@@ -203,20 +200,21 @@
     first = True
     for c in order:
         for k in range(1, peers):
-            pull(k, c).wait()
+            if first:
+                pull(k).wait()
 
             def fill(at, k=k):
                 snd[k - 1, :, pl.ds(at, edge), :] = term(k, at)
 
             tiles(c, fill)
-            if first:
+            if first and k == 1:
                 pl.semaphore_wait(barrier, peers + 1)
-                first = False
             start(share(k, c))
+        first = False
+    pull(0).wait()
     core_copy.wait()
 
     def gather(c):
-        pull(0, c).wait()
         for k in range(1, peers):
             share(k, c).wait_recv()
 
@@ -325,7 +323,7 @@
             pltpu.VMEM((nz + 4, wide + 2 * edge, deep), f32),
             pltpu.VMEM((nz + 4, wide, deep), f32),
             pltpu.VMEM((nz, wide + 2 * edge, deep), f32),
-            dma((peers, chunks)),
+            dma((peers,)),
             dma,
             dma((peers - 1, chunks)),
             dma((peers - 1, chunks)),
@@ -335,7 +333,7 @@
             dma((2, 2)),
         ],
         compiler_params=pltpu.CompilerParams(
-            collective_id=0, has_side_effects=True, vmem_limit_bytes=48 * 1024 * 1024
+            collective_id=0, has_side_effects=True, vmem_limit_bytes=67043328 - 640 * 1024
         ),
     )(states, occupations, core_density)
 

time: 35.6 us -> 32.7 us (0.919)
  local copies, waits for them, and re-layouts: 4.17 us -> 1.67 us
    unnamed x7 -> x1, local copies, waits for them, and re-layouts: 4.17 us -> 1.67 us
    pallas_call x1, Pallas kernels: 31.2 us -> 30.9 us  [shards(): pl.pallas_call(functools.partial(kernel, peers, slabs, rows), out_shape=j...]
where the time goes in v3:
time: 32.7 us; the launch traced here: 32.6 us
  Pallas kernels  30.9 us (94%)
  local copies, waits for them, and re-layouts  1.67 us (5%)
    pallas_call x1, Pallas kernels, shards(): pl.pallas_call(functools.partial(kernel, peers, slabs, rows), out_shape=j...  30.9 us
    unnamed x1, local copies, waits for them, and re-layouts  1.67 us

profile of v3, /device:TPU:0, one launch (start us, length us, event | category | flops | bytes accessed | tf_op | source)
XLA Modules:
  0.0 32.6 jit_solution(5425834648733060908)
XLA Ops:
  0.0 30.9 %shard_map.37 = f32[2,64,512]{2,1,0:T(8,128)} custom-call(f32[2,2,256,512]{3,2,1,0:T(8,128)} %states.1, s32[2]{0:T(128)} %occ.1, f32[2,256,512]{2,1,0:T(8,128)} %core.1), custom_call_target="tpu_custom_call" | custom-call | tf_op jit(solution)/shard_map/pallas_call | solution.py:309
  30.9 1.7 %copy.5 = f32[2,64,512]{2,1,0:T(8,128)} copy(f32[2,64,512]{2,1,0:T(8,128)} %shard_map.37) | data formatting | bytes 524288

commit v4 on v3

--- a/solution.py
+++ b/solution.py
@@ -302,7 +302,7 @@
 def shards(peers, slabs, states, occupations, core_density):
     nst, nz, full, deep = states.shape
     wide = full // peers
-    rows = 16 if wide % 16 == 0 else 8
+    rows = 32 if wide % 32 == 0 else 8
     chunks = wide // rows
     f32 = jnp.float32
     dma = pltpu.SemaphoreType.DMA
@@ -333,7 +333,7 @@
             dma((2, 2)),
         ],
         compiler_params=pltpu.CompilerParams(
-            collective_id=0, has_side_effects=True, vmem_limit_bytes=67043328 - 640 * 1024
+            collective_id=0, has_side_effects=True, vmem_limit_bytes=67043328 - 1000 * 1024
         ),
     )(states, occupations, core_density)
 

time: 32.7 us -> 32.8 us (level)
  the two profiles are of different devices: /device:TPU:0 before, /device:TPU:1 now
where the time goes in v4:
time: 32.8 us; the launch traced here: 32.7 us
  Pallas kernels  31 us (95%)
  local copies, waits for them, and re-layouts  1.67 us (5%)
    pallas_call x1, Pallas kernels, shards(): pl.pallas_call(functools.partial(kernel, peers, slabs, rows), out_shape=j...  31 us
    unnamed x1, local copies, waits for them, and re-layouts  1.67 us

profile of v4, /device:TPU:1, one launch (start us, length us, event | category | flops | bytes accessed | tf_op | source)
XLA Modules:
  0.0 32.7 jit_solution(2883155802496322360)
XLA Ops:
  0.0 31.0 %shard_map.37 = f32[2,64,512]{2,1,0:T(8,128)} custom-call(f32[2,2,256,512]{3,2,1,0:T(8,128)} %states.1, s32[2]{0:T(128)} %occ.1, f32[2,256,512]{2,1,0:T(8,128)} %core.1), custom_call_target="tpu_custom_call" | custom-call | tf_op jit(solution)/shard_map/pallas_call | solution.py:309
  31.0 1.7 %copy.5 = f32[2,64,512]{2,1,0:T(8,128)} copy(f32[2,64,512]{2,1,0:T(8,128)} %shard_map.37) | data formatting | bytes 524288

commit v5 on v3

--- a/solution.py
+++ b/solution.py
@@ -310,9 +310,9 @@
         functools.partial(kernel, peers, slabs, rows),
         out_shape=jax.ShapeDtypeStruct((nz, wide, deep), f32),
         in_specs=[
-            pl.BlockSpec(memory_space=pl.ANY),
+            pl.BlockSpec(memory_space=pltpu.HBM),
             pl.BlockSpec(memory_space=pltpu.SMEM),
-            pl.BlockSpec(memory_space=pl.ANY),
+            pl.BlockSpec(memory_space=pltpu.HBM),
         ],
         out_specs=pl.BlockSpec(memory_space=pltpu.VMEM),
         scratch_shapes=[
@@ -333,7 +333,7 @@
             dma((2, 2)),
         ],
         compiler_params=pltpu.CompilerParams(
-            collective_id=0, has_side_effects=True, vmem_limit_bytes=67043328 - 640 * 1024
+            collective_id=0, has_side_effects=True, vmem_limit_bytes=48 * 1024 * 1024
         ),
     )(states, occupations, core_density)
 

time: 32.7 us -> 35 us (1.070)
  local copies, waits for them, and re-layouts: 1.67 us -> 4.17 us
    unnamed x1 -> x7, local copies, waits for them, and re-layouts: 1.67 us -> 4.17 us
where the time goes in v5:
time: 35 us; the launch traced here: 34.8 us
  Pallas kernels  30.6 us (87%)
  local copies, waits for them, and re-layouts  4.17 us (12%)
    pallas_call x1, Pallas kernels, shards(): pl.pallas_call(functools.partial(kernel, peers, slabs, rows), out_shape=j...  30.6 us
    unnamed x7, local copies, waits for them, and re-layouts  4.17 us

profile of v5, /device:TPU:0, one launch (start us, length us, event | category | flops | bytes accessed | tf_op | source)
XLA Modules:
  0.0 34.8 jit_solution(18304583703536238864)
XLA Ops:
  0.0 0.0 copy-start
  0.0 1.6 %copy-done = f32[2,2,256,512]{3,2,1,0:T(8,128)S(1)} copy-done((f32[2,2,256,512]{3,2,1,0:T(8,128)S(1)}, f32[2,2,256,512]{3,2,1,0:T(8,128)}, u32[]{:S(2)}) %copy-start) | copy-done | bytes 2097176
  1.6 0.0 copy-start.1
  1.6 1.2 %copy-done.1 = f32[2,256,512]{2,1,0:T(8,128)S(1)} copy-done((f32[2,256,512]{2,1,0:T(8,128)S(1)}, f32[2,256,512]{2,1,0:T(8,128)}, u32[]{:S(2)}) %copy-start.1) | copy-done | bytes 1048600
  2.8 0.0 copy-start.2
  2.8 0.7 %copy-done.2 = s32[2]{0:T(128)S(1)} copy-done((s32[2]{0:T(128)S(1)}, s32[2]{0:T(128)}, u32[]{:S(2)}) %copy-start.2) | copy-done | bytes 32
  3.5 30.6 %shard_map.37 = f32[2,64,512]{2,1,0:T(8,128)S(1)} custom-call(f32[2,2,256,512]{3,2,1,0:T(8,128)S(1)} %copy-done, s32[2]{0:T(128)S(1)} %copy-done.2, f32[2,256,512]{2,1,0:T(8,128)S(1)} %copy-done.1), custom_call_target="tpu_custom_call" | custom-call | tf_op jit(solution)/shard_map/pallas_call | solution.py:309
  34.1 0.7 %copy.5 = f32[2,64,512]{2,1,0:T(8,128)} copy(f32[2,64,512]{2,1,0:T(8,128)S(1)} %shard_map.37) | data formatting | bytes 524288
Async XLA Ops:
  0.0 1.6 %copy-start = (f32[2,2,256,512]{3,2,1,0:T(8,128)S(1)}, f32[2,2,256,512]{3,2,1,0:T(8,128)}, u32[]{:S(2)}) copy-start(f32[2,2,256,512]{3,2,1,0:T(8,128)} %states.1) | copy-start | bytes 6291460
  1.6 1.2 %copy-start.1 = (f32[2,256,512]{2,1,0:T(8,128)S(1)}, f32[2,256,512]{2,1,0:T(8,128)}, u32[]{:S(2)}) copy-start(f32[2,256,512]{2,1,0:T(8,128)} %core.1) | copy-start | bytes 3145732
  2.8 0.7 %copy-start.2 = (s32[2]{0:T(128)S(1)}, s32[2]{0:T(128)}, u32[]{:S(2)}) copy-start(s32[2]{0:T(128)} %occ.1) | copy-start | bytes 28

commit v6 on v3

--- a/solution.py
+++ b/solution.py
@@ -103,8 +103,8 @@
 def kernel(
     peers, slabs, rows,
     states, occ, core, out,
-    stage, core_v, snd, rcv, dens, fz, fx,
-    in_sem, core_sem, rs_send, rs_recv, z_send, z_recv, x_send, x_recv,
+    stage, core_v, snd, rcv, pair_out, pair_in, dens, fz, fx,
+    in_sem, core_sem, rs_send, rs_recv, pair_send, pair_recv, z_send, z_recv, x_send, x_recv,
 ):
     nst, nz, wide = stage.shape[1], stage.shape[2], stage.shape[3]
     chunks = wide // rows
@@ -114,10 +114,16 @@
     z_high = lax.rem(sl + 1, slabs)
     x_low = lax.rem(me + peers - 1, peers)
     x_high = lax.rem(me + 1, peers)
+    square = peers == 4
+    if square:
+        hi, lo = lax.div(me, 2), lax.rem(me, 2)
+        peer = [me, me + 1 - 2 * lo, me + 2 - 4 * hi, 3 - me]
+    else:
+        peer = [lax.rem(me + k, peers) for k in range(peers)]
     order = [0] + ([chunks - 1] if chunks > 1 else []) + list(range(1, chunks - 1))
 
     def pull(k):
-        start = pl.multiple_of(lax.rem(me + k, peers) * wide, 8)
+        start = pl.multiple_of(peer[k] * wide, 8)
         return pltpu.make_async_copy(
             states.at[:, :, pl.ds(start, wide), :], stage.at[k], in_sem.at[k]
         )
@@ -132,7 +138,7 @@
     barrier = pltpu.get_barrier_semaphore()
     for k in range(1, peers):
         pl.semaphore_signal(
-            barrier, inc=1, device_id=(lax.rem(me + k, peers), sl), device_id_type=MESH
+            barrier, inc=1, device_id=(peer[k], sl), device_id_type=MESH
         )
     for z in (z_low, z_high):
         pl.semaphore_signal(barrier, inc=1, device_id=(me, z), device_id_type=MESH)
@@ -161,7 +167,7 @@
             dst_ref=rcv.at[k - 1, :, span, :],
             send_sem=rs_send.at[k - 1, c],
             recv_sem=rs_recv.at[k - 1, c],
-            device_id=(lax.rem(me + k, peers), sl),
+            device_id=(peer[k], sl),
             device_id_type=MESH,
         )
 
@@ -197,8 +203,46 @@
         copy.start()
         started.append(copy)
 
-    first = True
-    for c in order:
+    def near(c):
+        return 1 + order.index(c) % 2
+
+    def both(c):
+        return pltpu.make_async_remote_copy(
+            src_ref=pair_out.at[c],
+            dst_ref=pair_in.at[c],
+            send_sem=pair_send.at[c],
+            recv_sem=pair_recv.at[c],
+            device_id=(peer[near(c)], sl),
+            device_id_type=MESH,
+        )
+
+    def relay(c):
+        both(c).wait_recv()
+        k = 3 - near(c)
+
+        def fill(at):
+            passed = pair_in[c, 1, :, pl.ds(pl.multiple_of(at - c * rows, edge), edge), :]
+            snd[k - 1, :, pl.ds(at, edge), :] = term(k, at) + passed
+
+        tiles(c, fill)
+        start(share(k, c))
+
+    if square:
+        for k in range(1, peers):
+            pull(k).wait()
+        for c in order:
+
+            def fill(at, c=c):
+                here = pl.ds(pl.multiple_of(at - c * rows, edge), edge)
+                pair_out[c, 0, :, here, :] = term(near(c), at)
+                pair_out[c, 1, :, here, :] = term(3, at)
+
+            tiles(c, fill)
+            if c == order[0]:
+                pl.semaphore_wait(barrier, peers + 1)
+            start(both(c))
+    first = not square
+    for c in [] if square else order:
         for k in range(1, peers):
             if first:
                 pull(k).wait()
@@ -215,12 +259,15 @@
     core_copy.wait()
 
     def gather(c):
-        for k in range(1, peers):
+        arrived = [3 - near(c)] if square else list(range(1, peers))
+        for k in arrived:
             share(k, c).wait_recv()
 
         def add(at):
             total = term(0, at)
-            for k in range(1, peers):
+            if square:
+                total = total + pair_in[c, 0, :, pl.ds(pl.multiple_of(at - c * rows, edge), edge), :]
+            for k in arrived:
                 total = total + rcv[k - 1, :, pl.ds(at, edge), :]
             dens[2 : nz + 2, pl.ds(at + edge, edge), :] = (
                 total + core_v[:, pl.ds(at, edge), :]
@@ -280,13 +327,18 @@
         tiles(c, work)
 
     gathered, done = set(), set()
-    for c in order:
+    ahead = list(order) if square else []
+    for c in ahead[:2]:
+        relay(c)
+    for i, c in enumerate(order):
+        for later in ahead[2:] if i == 0 else []:
+            relay(later)
         gather(c)
         gathered.add(c)
         for d in order:
-            near = {e for e in (d - 1, d, d + 1) if 0 <= e < chunks}
+            around = {e for e in (d - 1, d, d + 1) if 0 <= e < chunks}
             ends = d not in (0, chunks - 1) or {0, chunks - 1} <= gathered
-            if d not in done and near <= gathered and ends and len(gathered) > 2:
+            if d not in done and around <= gathered and ends and len(gathered) > 2:
                 energy(d)
                 done.add(d)
                 break
@@ -320,6 +372,8 @@
             pltpu.VMEM((nz, wide, deep), f32),
             pltpu.VMEM((peers - 1, nz, wide, deep), f32),
             pltpu.VMEM((peers - 1, nz, wide, deep), f32),
+            pltpu.VMEM((chunks, 2, nz, rows, deep), f32),
+            pltpu.VMEM((chunks, 2, nz, rows, deep), f32),
             pltpu.VMEM((nz + 4, wide + 2 * edge, deep), f32),
             pltpu.VMEM((nz + 4, wide, deep), f32),
             pltpu.VMEM((nz, wide + 2 * edge, deep), f32),
@@ -327,6 +381,8 @@
             dma,
             dma((peers - 1, chunks)),
             dma((peers - 1, chunks)),
+            dma((chunks,)),
+            dma((chunks,)),
             dma((2, 2, chunks)),
             dma((2, 2, chunks)),
             dma((2, 2)),

time: 32.7 us -> 32.6 us (level)
  no operation moved by 1% of the time
where the time goes in v6:
time: 32.6 us; the launch traced here: 32.4 us
  Pallas kernels  30.7 us (94%)
  local copies, waits for them, and re-layouts  1.67 us (5%)
    pallas_call x1, Pallas kernels, shards(): pl.pallas_call(functools.partial(kernel, peers, slabs, rows), out_shape=j...  30.7 us
    unnamed x1, local copies, waits for them, and re-layouts  1.67 us

profile of v6, /device:TPU:0, one launch (start us, length us, event | category | flops | bytes accessed | tf_op | source)
XLA Modules:
  0.0 32.4 jit_solution(13078159918235381618)
XLA Ops:
  0.0 30.7 %shard_map.37 = f32[2,64,512]{2,1,0:T(8,128)} custom-call(f32[2,2,256,512]{3,2,1,0:T(8,128)} %states.1, s32[2]{0:T(128)} %occ.1, f32[2,256,512]{2,1,0:T(8,128)} %core.1), custom_call_target="tpu_custom_call" | custom-call | tf_op jit(solution)/shard_map/pallas_call | solution.py:361
  30.7 1.7 %copy.5 = f32[2,64,512]{2,1,0:T(8,128)} copy(f32[2,64,512]{2,1,0:T(8,128)} %shard_map.37) | data formatting | bytes 524288

commit v7 on v6

--- a/solution.py
+++ b/solution.py
@@ -240,7 +240,8 @@
             tiles(c, fill)
             if c == order[0]:
                 pl.semaphore_wait(barrier, peers + 1)
-            start(both(c))
+            if c in order[:2]:
+                start(both(c))
     first = not square
     for c in [] if square else order:
         for k in range(1, peers):
@@ -330,8 +331,10 @@
     ahead = list(order) if square else []
     for c in ahead[:2]:
         relay(c)
+    for c in ahead[2:]:
+        start(both(c))
     for i, c in enumerate(order):
-        for later in ahead[2:] if i == 0 else []:
+        for later in ahead[2:] if i == 2 else []:
             relay(later)
         gather(c)
         gathered.add(c)

time: 32.6 us -> 32.7 us (level)
  no operation moved by 1% of the time
where the time goes in v7:
time: 32.7 us; the launch traced here: 32.5 us
  Pallas kernels  30.8 us (94%)
  local copies, waits for them, and re-layouts  1.67 us (5%)
    pallas_call x1, Pallas kernels, shards(): pl.pallas_call(functools.partial(kernel, peers, slabs, rows), out_shape=j...  30.8 us
    unnamed x1, local copies, waits for them, and re-layouts  1.67 us

profile of v7, /device:TPU:0, one launch (start us, length us, event | category | flops | bytes accessed | tf_op | source)
XLA Modules:
  0.0 32.5 jit_solution(4471415450529924911)
XLA Ops:
  0.0 30.8 %shard_map.37 = f32[2,64,512]{2,1,0:T(8,128)} custom-call(f32[2,2,256,512]{3,2,1,0:T(8,128)} %states.1, s32[2]{0:T(128)} %occ.1, f32[2,256,512]{2,1,0:T(8,128)} %core.1), custom_call_target="tpu_custom_call" | custom-call | tf_op jit(solution)/shard_map/pallas_call | solution.py:364
  30.8 1.7 %copy.5 = f32[2,64,512]{2,1,0:T(8,128)} copy(f32[2,64,512]{2,1,0:T(8,128)} %shard_map.37) | data formatting | bytes 524288
